TPU v7x, 32 devices: a whole 2x2x4 slice. The times are simulated.
32 devices in a mesh: dp: 2 (over y), space: 4 (over z), chan: 4 (over x, core).
Axes of the slice: x: 2, y: 2, z: 4, core: 2. Of those that a mesh axis runs over, the one named last changes fastest.
Arguments:
- volumes: bfloat16 [2, 8, 512, 1024], P('dp', 'space', 'chan'), may hold values from -6 to 6
- kernel: bfloat16 [512, 13824], P('chan'), may hold values from -0.15625 to 0.15625
- bias: float32 [512], P('chan'), may hold values from -3 to 3
- act_grad: bfloat16 [2, 4, 512, 256], P('dp', 'space', 'chan'), may hold values from -6 to 6
Outputs:
- activation: bfloat16 [2, 4, 512, 256], P('dp', 'space', 'chan')
- grad_x: bfloat16 [2, 8, 512, 1024], P('dp', 'space', 'chan')
- grad_w: float32 [512, 13824], P('chan')
- grad_b: float32 [512], P('chan')
All inputs are finite; a program needn't handle non-finite values.
Results may differ from a plain program's by a relative error of at most 0.005.
Values may be sent and summed in bfloat16 or wider, within the bound.
A program may use at most 64 MiB of HBM per device.

v0:
```python
import functools

import jax
import jax.numpy as jnp
from jax import lax
from jax.experimental import pallas as pl
from jax.experimental.pallas import tpu as pltpu
from jax.sharding import PartitionSpec as P

GRID = 32
HALF = GRID // 2
CELLS = HALF * HALF
BF = jnp.bfloat16
F32 = jnp.float32
VM = pl.BlockSpec(memory_space=pltpu.VMEM)
TAPS = [(k1, k2, k3) for k1 in range(3) for k2 in range(3) for k3 in range(3)]


def phase_of(k2, k3):
    return 2 * (k2 != 1) + (k3 != 1)


def shift_of(k2, k3):
    return 2 * (k2 == 0) + (k3 == 0)


def parity_matrix():
    full = GRID * GRID
    dst = lax.broadcasted_iota(jnp.int32, (1, full), 1)
    phase, cell = dst // CELLS, dst % CELLS
    y = 2 * (cell // HALF) + phase // 2
    z = 2 * (cell % HALF) + phase % 2
    src = y * GRID + z
    rows = lax.broadcasted_iota(jnp.int32, (full, full), 0)
    return jnp.where(rows == src, 1.0, 0.0).astype(BF)


def lanes():
    return lax.broadcasted_iota(jnp.int32, (1, CELLS), 1)


def forward_shift(x, s):
    if s & 2:
        x = jnp.where(lanes() >= HALF, pltpu.roll(x, HALF, 1), 0.0)
    if s & 1:
        x = jnp.where(lanes() % HALF != 0, pltpu.roll(x, 1, 1), 0.0)
    return x


def backward_shift(x, s):
    if s & 2:
        x = jnp.where(lanes() < CELLS - HALF, pltpu.roll(x, CELLS - HALF, 1), 0.0)
    if s & 1:
        x = jnp.where(lanes() % HALF != HALF - 1, pltpu.roll(x, CELLS - 1, 1), 0.0)
    return x


def split_kernel(v_ref, p_ref, o_ref):
    o_ref[...] = jnp.dot(v_ref[...], p_ref[...], preferred_element_type=F32).astype(BF)


def merge_kernel(v_ref, p_ref, o_ref):
    o_ref[...] = lax.dot_general(
        v_ref[...], p_ref[...], (((1,), (1,)), ((), ())), preferred_element_type=F32
    ).astype(BF)


def forward_kernel(width, x_ref, w_ref, b_ref, g_ref, act_ref, dy_ref, db_ref):
    sums = [None] * 4
    for t, (k1, k2, k3) in enumerate(TAPS):
        ph, s = phase_of(k2, k3), shift_of(k2, k3)
        part = jnp.dot(
            w_ref[:, t * width : (t + 1) * width],
            x_ref[k1, :, ph * CELLS : (ph + 1) * CELLS],
            preferred_element_type=F32,
        )
        sums[s] = part if sums[s] is None else sums[s] + part
    u = b_ref[...] + sums[0]
    for s in (1, 2, 3):
        u = u + forward_shift(sums[s], s)
    c = 0.7978845608028654
    th = jnp.tanh(c * (u + 0.044715 * (u * u * u)))
    act_ref[...] = (0.5 * u * (1.0 + th)).astype(BF)
    slope = 0.5 * (1.0 + th) + 0.5 * u * (1.0 - th * th) * c * (1.0 + 3 * 0.044715 * u * u)
    dy = (g_ref[...].astype(F32) * slope).astype(BF)
    dy_ref[...] = dy
    db_ref[...] = jnp.sum(dy.astype(F32), axis=1, keepdims=True)


def shifted(dy):
    wide = dy.astype(F32)
    return [dy] + [backward_shift(wide, s).astype(BF) for s in (1, 2, 3)]


def weight_kernel(width, x_ref, dy_ref, dw_ref):
    views = shifted(dy_ref[...])
    for t, (k1, k2, k3) in enumerate(TAPS):
        ph, s = phase_of(k2, k3), shift_of(k2, k3)
        part = lax.dot_general(
            views[s],
            x_ref[k1, :, ph * CELLS : (ph + 1) * CELLS],
            (((1,), (1,)), ((), ())),
            preferred_element_type=F32,
        )
        dw_ref[:, t * width : (t + 1) * width] = part.astype(BF)


def input_kernel(width, w_ref, dy_ref, next_ref, gx_ref):
    own = shifted(dy_ref[...])
    following = shifted(next_ref[...])
    for plane in range(2):
        for ph in range(4):
            total = None
            for t, (k1, k2, k3) in enumerate(TAPS):
                if phase_of(k2, k3) != ph or (k1 == 1) != (plane == 0):
                    continue
                views = following if k1 == 0 else own
                part = lax.dot_general(
                    w_ref[:, t * width : (t + 1) * width],
                    views[shift_of(k2, k3)],
                    (((0,), (0,)), ((), ())),
                    preferred_element_type=F32,
                )
                total = part if total is None else total + part
            gx_ref[plane, :, ph * CELLS : (ph + 1) * CELLS] = total.astype(BF)


def call(kernel, out_shape, n_in, flops, moved):
    many = isinstance(out_shape, (tuple, list))
    return pl.pallas_call(
        kernel,
        out_shape=out_shape,
        in_specs=[VM] * n_in,
        out_specs=[VM] * len(out_shape) if many else VM,
        compiler_params=pltpu.CompilerParams(vmem_limit_bytes=48 << 20),
        cost_estimate=pl.CostEstimate(flops=flops, bytes_accessed=moved, transcendentals=0),
    )


def shape(*dims, dtype=BF):
    return jax.ShapeDtypeStruct(dims, dtype)


def from_behind(array, axis, by):
    size = lax.axis_size(axis)
    pairs = [(i, i + by) for i in range(size) if 0 <= i + by < size]
    return lax.ppermute(array, axis, pairs)


def per_device(volumes, kernel, bias, act_grad):
    batch, planes, part, cells = volumes.shape
    filters = kernel.shape[0]
    width = kernel.shape[1] // 27
    parity = parity_matrix()
    own = call(split_kernel, shape(planes * part, cells), 2, 2 * planes * part * cells**2, 1 << 20)(
        volumes.reshape(planes * part, cells), parity
    ).reshape(planes, part, cells)
    rim = from_behind(own[-1:], "space", 1)
    x_all = lax.all_gather(jnp.concatenate([rim, own], 0), "chan", axis=1, tiled=True)
    flops = 2 * 27 * width * filters * CELLS
    act, dy, db = call(
        functools.partial(forward_kernel, width),
        (shape(filters, CELLS), shape(filters, CELLS), shape(filters, 1, dtype=F32)),
        4,
        flops,
        7 << 20,
    )(x_all, kernel, bias.reshape(filters, 1), act_grad.reshape(filters, CELLS))
    dy_next = from_behind(dy, "space", -1)
    dw = call(functools.partial(weight_kernel, width), shape(filters, 27 * width), 2, flops, 7 << 20)(
        x_all, dy
    )
    gx = call(functools.partial(input_kernel, width), shape(planes, width, cells), 3, 2 * flops, 6 << 20)(
        kernel, dy, dy_next
    )
    count = batch * lax.axis_size("dp")
    dw_sum = lax.psum_scatter(dw, ("dp", "space"), scatter_dimension=0, tiled=True)
    dw_all = lax.all_gather(dw_sum, ("dp", "space"), axis=0, tiled=True)
    grad_w = dw_all.astype(F32) / count
    grad_b = lax.psum(db[:, 0], ("dp", "space")) / count
    gx_sum = lax.psum_scatter(gx, "chan", scatter_dimension=1, tiled=True)
    grad_x = call(merge_kernel, shape(planes * part, cells), 2, 2 * planes * part * cells**2, 1 << 20)(
        gx_sum.reshape(planes * part, cells), parity
    )
    return (
        act.reshape(act_grad.shape),
        grad_x.reshape(volumes.shape),
        grad_w,
        grad_b,
    )


def solution(mesh):
    in_specs = (
        P("dp", "space", "chan", None),
        P("chan", None),
        P("chan"),
        P("dp", "space", "chan", None),
    )
    out_specs = (
        P("dp", "space", "chan", None),
        P("dp", "space", "chan", None),
        P("chan", None),
        P("chan"),
    )
    return jax.shard_map(
        per_device, mesh=mesh, in_specs=in_specs, out_specs=out_specs, check_vma=False
    )
```

profile of v0, /device:TPU:0, one launch (start us, length us, event | category | flops | bytes accessed | tf_op | source)
XLA Modules:
  0.0 254.1 jit_solution(16425274963394763646)
XLA Ops:
  7.2 0.0 all-gather.3.cloned.1.call-start
  7.2 0.9 select_convert_fusion.p_ref
  8.1 1.0 copy-done.3
  9.2 0.7 shard_map.75
  9.9 5.0 %collective-permute-start = (bf16[1,128,1024]{2,1,0:T(8,128)(2,1)S(1)}, bf16[1,128,1024]{2,1,0:T(8,128)(2,1)S(1)}, u32[]{:S(2)}, u32[]{:S(2)}) collective-permute-start(bf16[1,128,1024]{2,1,0:T(8,128)(2,1)S(1)} %slice_bitcast_fusion), channel_id=1, source_target_pairs={{0,4},{4,8},{8,12},{1,5},{5,9},{9,13},{2,6},{6,10},{10,14},{3,7},{... | collective-permute-start | bytes 786440 | tf_op jit(solution)/shard_map/ppermute | solution.py:147
  14.9 5.5 %collective-permute-done = bf16[1,128,1024]{2,1,0:T(8,128)(2,1)S(1)} collective-permute-done((bf16[1,128,1024]{2,1,0:T(8,128)(2,1)S(1)}, bf16[1,128,1024]{2,1,0:T(8,128)(2,1)S(1)}, u32[]{:S(2)}, u32[]{:S(2)}) %collective-permute-start) | collective-permute-done | bytes 262176 | tf_op jit(solution)/shard_map/ppermute | solution.py:147
  20.4 0.9 pad_maximum_fusion
  21.4 0.0 all-gather.3.cloned.1.call-update
  21.4 0.0 reduce-scatter.5.cloned.1.call-start
  21.5 0.1 copy.9.b_ref
  21.6 30.6 %all-gather.3.cloned.1.call-done.x_ref = bf16[3,512,1024]{2,1,0:T(8,128)(2,1)} async-done(((bf16[3,128,1024]{2,1,0:T(8,128)(2,1)}), bf16[3,512,1024]{2,1,0:T(8,128)(2,1)}) %all-gather.3.cloned.1.call-update) | async-done | bytes 3145744 | tf_op jit(solution)/shard_map/all_gather | solution.py:159
  52.2 1.9 copy-done
  54.1 3.9 %shard_map.76 = (bf16[128,256]{1,0:T(8,128)(2,1)}, bf16[128,256]{1,0:T(8,128)(2,1)S(1)}, f32[128,1]{1,0:T(8,128)S(1)}) custom-call(bf16[3,512,1024]{2,1,0:T(8,128)(2,1)S(1)} %copy-done, bf16[128,13824]{1,0:T(8,128)(2,1)} %w_ref.3, f32[128,1]{1,0:T(8,128)S(1)} %copy.9.b_ref, bf16[128,256]{1,0:T(8,128)(2,1)S(1)} %bitcast.12), custom_call_target="tpu_custom_call" | custom-call | flops 905969664 | bytes 7340032 | tf_op jit(solution)/shard_map/pallas_call | solution.py:161
  58.0 4.3 %shard_map.79 = bf16[128,13824]{1,0:T(8,128)(2,1)} custom-call(bf16[3,512,1024]{2,1,0:T(8,128)(2,1)S(1)} %copy-done, bf16[128,256]{1,0:T(8,128)(2,1)S(1)} %get-tuple-element.8.dy_ref), custom_call_target="tpu_custom_call" | custom-call | flops 905969664 | bytes 7340032 | tf_op jit(solution)/shard_map/pallas_call | solution.py:169
  62.4 0.0 reduce-scatter.3.cloned.1.call-start
  62.4 1.3 collective-permute-start.1
  63.7 4.9 %collective-permute-done.1.next_ref = bf16[128,256]{1,0:T(8,128)(2,1)S(1)} collective-permute-done((bf16[128,256]{1,0:T(8,128)(2,1)S(1)}, bf16[128,256]{1,0:T(8,128)(2,1)S(1)}, u32[]{:S(2)}, u32[]{:S(2)}) %collective-permute-start.1) | collective-permute-done | bytes 65568 | tf_op jit(solution)/shard_map/ppermute | solution.py:147
  68.6 2.3 copy-done.1
  70.9 2.0 shard_map.77
  72.9 1.3 copy-done.2
  74.3 0.0 reduce-scatter.3.cloned.1.call-update
  74.3 0.0 all-gather.5.cloned.1.call-start
  74.3 67.6 %reduce-scatter.5.cloned.1.call-done = bf16[16,13824]{1,0:T(8,128)(2,1)} async-done(((bf16[128,13824]{1,0:T(8,128)(2,1)}), bf16[16,13824]{1,0:T(8,128)(2,1)}) %reduce-scatter.5.cloned.1.call-update) | async-done | bytes 442384 | tf_op jit(solution)/shard_map/reduce_scatter | solution.py:176
  142.0 0.0 all-gather.5.cloned.1.call-update
  142.0 0.1 reduce
  142.1 20.2 %psum.7 = f32[128]{0:T(128)S(1)} all-reduce(f32[128]{0:T(128)S(1)} %reduce), channel_id=1, replica_groups=mesh['dp'=2,'space'=4,'chan'=4] {'dp','space'}, use_global_device_ids=true, to_apply=%region_2.3 | all-reduce | flops 128 | bytes 1024 | tf_op jit(solution)/shard_map/psum | solution.py:179
  162.3 0.5 broadcast_multiply_fusion
  162.8 12.5 %reduce-scatter.3.cloned.1.call-done = bf16[2,128,1024]{2,1,0:T(8,128)(2,1)} async-done(((bf16[2,512,1024]{2,1,0:T(8,128)(2,1)}), bf16[2,128,1024]{2,1,0:T(8,128)(2,1)}) %reduce-scatter.3.cloned.1.call-update) | async-done | bytes 524304 | tf_op jit(solution)/shard_map/reduce_scatter | solution.py:180
  175.3 1.0 copy-done.4
  176.4 1.5 shard_map.78
  177.9 64.0 %all-gather.5.cloned.1.call-done = bf16[128,13824]{1,0:T(8,128)(2,1)} async-done(((bf16[16,13824]{1,0:T(8,128)(2,1)}), bf16[128,13824]{1,0:T(8,128)(2,1)}) %all-gather.5.cloned.1.call-update) | async-done | bytes 3538960 | tf_op jit(solution)/shard_map/all_gather | solution.py:177
  241.9 5.7 %convert_multiply_fusion = f32[128,13824]{1,0:T(8,128)} fusion(bf16[128,13824]{1,0:T(8,128)(2,1)} %all-gather.5.cloned.1.call-done), kind=kLoop, calls=%fused_computation | loop fusion | flops 3538944 | bytes 10616832 | tf_op jit(solution)/shard_map/div | solution.py:178
  (12 shorter events, 0.1 us)
Async XLA Ops:
  7.2 14.3 %copy-start.6 = (f32[128]{0:T(128)S(1)}, f32[128]{0:T(128)}, u32[]{:S(2)}) copy-start(f32[128]{0:T(128)} %param.6) | copy-start | bytes 1540
  7.2 45.0 %copy-start.5 = (bf16[1,1,128,256]{3,2,1,0:T(8,128)(2,1)S(1)}, bf16[1,1,128,256]{3,2,1,0:T(8,128)(2,1)}, u32[]{:S(2)}) copy-start(bf16[1,1,128,256]{3,2,1,0:T(8,128)(2,1)} %param.7) | copy-start | bytes 196612
  7.2 45.0 %all-gather.3.cloned.1.call-start = ((), (), s32[]{:S(2)}) async-start(), calls=%async_computation.2 | async-start | bytes 3932160 | tf_op jit(solution)/shard_map/all_gather | solution.py:159
  8.1 1.0 copy-start.3
  9.9 10.5 %collective-permute-start = (bf16[1,128,1024]{2,1,0:T(8,128)(2,1)S(1)}, bf16[1,128,1024]{2,1,0:T(8,128)(2,1)S(1)}, u32[]{:S(2)}, u32[]{:S(2)}) collective-permute-start(bf16[1,128,1024]{2,1,0:T(8,128)(2,1)S(1)} %slice_bitcast_fusion), channel_id=1, source_target_pairs={{0,4},{4,8},{8,12},{1,5},{5,9},{9,13},{2,6},{6,10},{10,14},{3,7},{... | collective-permute-start | bytes 786440 | tf_op jit(solution)/shard_map/ppermute | solution.py:147
  21.4 120.6 %reduce-scatter.5.cloned.1.call-start = ((), (), s32[]{:S(2)}) async-start(), calls=%async_computation.4 | async-start | bytes 3981312 | tf_op jit(solution)/shard_map/reduce_scatter | solution.py:176
  52.2 1.9 copy-start
  62.4 113.0 %reduce-scatter.3.cloned.1.call-start = ((), (), s32[]{:S(2)}) async-start(), calls=%async_computation.3 | async-start | bytes 2621440 | tf_op jit(solution)/shard_map/reduce_scatter | solution.py:180
  62.4 6.2 %collective-permute-start.1 = (bf16[128,256]{1,0:T(8,128)(2,1)S(1)}, bf16[128,256]{1,0:T(8,128)(2,1)S(1)}, u32[]{:S(2)}, u32[]{:S(2)}) collective-permute-start(bf16[128,256]{1,0:T(8,128)(2,1)S(1)} %get-tuple-element.8.dy_ref), channel_id=1, source_target_pairs={{4,0},{8,4},{12,8},{5,1},{9,5},{13,9},{6,2},{10,6},{14,10},{7,3},{... | collective-permute-start | bytes 196616 | tf_op jit(solution)/shard_map/ppermute | solution.py:147
  68.6 2.3 copy-start.1
  72.9 1.4 copy-start.2
  74.3 167.6 %all-gather.5.cloned.1.call-start = ((), (), s32[]{:S(2)}) async-start(), calls=%async_computation.5 | async-start | bytes 3981312 | tf_op jit(solution)/shard_map/all_gather | solution.py:177
  175.3 1.0 copy-start.4
Sparse Core Ops, SparseCore 0:
  21.5 30.6 all-gather.2
  62.5 79.4 reduce-scatter.4
  144.5 30.7 reduce-scatter.2
  177.3 64.5 all-gather.4
where the time goes:
time: 255 us; the launch traced here: 254 us
  waiting for transfers between devices  185 us (73%)
  blocking collectives  20.2 us (8%)
  between operations  13.9 us (5%)
  Pallas kernels  12.5 us (5%)
  other arithmetic  8.13 us (3%)
  local copies, waits for them, and re-layouts  7.76 us (3%)
  starting transfers between devices  6.43 us (3%)
    reduce_scatter x1, waiting for transfers between devices, per_device(): lax.psum_scatter(dw, ('dp', 'space'), scatter_dimension=0, tiled=True)  67.6 us
    all_gather x1, waiting for transfers between devices, per_device(): dw_all = lax.all_gather(dw_sum, ('dp', 'space'), axis=0, tiled=True)  64 us
    all_gather x1, waiting for transfers between devices, per_device(): lax.all_gather(jnp.concatenate([rim, own], 0), 'chan', axis=1, tiled=True)  30.6 us
    psum x1, blocking collectives, per_device(): grad_b = lax.psum(db[:, 0], ('dp', 'space')) / count  20.2 us
    reduce_scatter x1, waiting for transfers between devices, per_device(): gx_sum = lax.psum_scatter(gx, 'chan', scatter_dimension=1, tiled=True)  12.5 us
    ppermute x2, waiting for transfers between devices, from_behind(): return lax.ppermute(array, axis, pairs)  10.4 us
    unnamed x14, local copies, waits for them, and re-layouts  7.63 us
    ppermute x2, starting transfers between devices, from_behind(): return lax.ppermute(array, axis, pairs)  6.26 us
  transfers between devices with their start and end apart: 6, of which 6 were waited for; matrix products, arithmetic and copies ran while one was open for 0% of the time, Pallas kernels for 1%

commit v1 on v0

--- a/solution.py
+++ b/solution.py
@@ -60,18 +60,134 @@
 
 
 def merge_kernel(v_ref, p_ref, o_ref):
+    total = v_ref[0].astype(F32)
+    for j in range(1, v_ref.shape[0]):
+        total = total + v_ref[j].astype(F32)
     o_ref[...] = lax.dot_general(
-        v_ref[...], p_ref[...], (((1,), (1,)), ((), ())), preferred_element_type=F32
+        total.astype(BF).reshape(o_ref.shape), p_ref[...], (((1,), (1,)), ((), ())), preferred_element_type=F32
     ).astype(BF)
 
 
-def forward_kernel(width, x_ref, w_ref, b_ref, g_ref, act_ref, dy_ref, db_ref):
+def send(src, dst, send_sem, recv_sem, device):
+    return pltpu.make_async_remote_copy(
+        src, dst, send_sem, recv_sem, device_id=device, device_id_type=pl.DeviceIdType.MESH
+    )
+
+
+def place():
+    return lax.axis_index("dp"), lax.axis_index("space"), lax.axis_index("chan")
+
+
+def greet(sizes):
+    n_dp, n_space, n_chan = sizes
+    y, z, c = place()
+    barrier = pltpu.get_barrier_semaphore()
+    g = y * n_space + z
+    for o in range(1, n_chan):
+        pl.semaphore_signal(
+            barrier, 1, device_id=(y, z, (c + o) % n_chan), device_id_type=pl.DeviceIdType.MESH
+        )
+    for o in range(1, n_dp * n_space):
+        h = (g + o) % (n_dp * n_space)
+        pl.semaphore_signal(
+            barrier, 1, device_id=(h // n_space, h % n_space, c), device_id_type=pl.DeviceIdType.MESH
+        )
+    pl.semaphore_wait(barrier, n_chan + n_dp * n_space - 2)
+
+
+def gather_inputs(sizes, own_ref, x_ref, out_sem, in_sem, local_sem):
+    n_dp, n_space, n_chan = sizes
+    chips = n_chan // 2
+    y, z, c = place()
+    chip, core = c // 2, c % 2
+    twin = (y, z, 2 * chip + 1 - core)
+    greet(sizes)
+
+    def planes(k):
+        return pl.ds(1, 2) if k else pl.ds(0, 1)
+
+    def block(k, j):
+        return x_ref.at[planes(k), j]
+
+    def to_chip(k, o, src):
+        return send(
+            src, block(k, c), out_sem.at[k, 0, o], in_sem.at[k, c],
+            (y, z, 2 * ((chip + o) % chips) + core),
+        )
+
+    def to_twin(k, o, src):
+        j = 2 * ((chip - o + chips) % chips) + core
+        return send(src, block(k, j), out_sem.at[k, 1, o], in_sem.at[k, j], twin)
+
+    def arrived(k, j):
+        send(block(k, j), block(k, j), out_sem.at[k, 1, 0], in_sem.at[k, j], twin).wait_recv()
+
+    rim = send(own_ref.at[pl.ds(1, 1)], block(0, c), out_sem.at[0, 2, 0], in_sem.at[0, c], (y, jnp.minimum(z + 1, n_space - 1), c))
+    sends = [to_chip(1, o, own_ref) for o in range(1, chips)] + [to_twin(1, 0, own_ref)]
+
+    @pl.when(z < n_space - 1)
+    def _():
+        rim.start()
+
+    for copy in sends:
+        copy.start()
+    keep = pltpu.make_async_copy(own_ref, block(1, c), local_sem)
+    keep.start()
+
+    rim_out = [to_chip(0, o, block(0, c)) for o in range(1, chips)] + [to_twin(0, 0, block(0, c))]
+
+    @pl.when(z > 0)
+    def _():
+        arrived(0, c)
+        for copy in rim_out:
+            copy.start()
+
+    @pl.when(z == 0)
+    def _():
+        x_ref[0] = jnp.zeros_like(x_ref[0])
+
+    for o in range(1, chips):
+        j = 2 * ((chip - o + chips) % chips) + core
+        arrived(1, j)
+        passed = to_twin(1, o, block(1, j))
+        passed.start()
+        sends.append(passed)
+
+    @pl.when(z > 0)
+    def _():
+        for o in range(1, chips):
+            j = 2 * ((chip - o + chips) % chips) + core
+            arrived(0, j)
+            passed = to_twin(0, o, block(0, j))
+            passed.start()
+            rim_out.append(passed)
+        for o in range(chips):
+            arrived(0, 2 * ((chip - o + chips) % chips) + 1 - core)
+        for copy in rim_out:
+            copy.wait_send()
+
+    for o in range(chips):
+        arrived(1, 2 * ((chip - o + chips) % chips) + 1 - core)
+    for copy in sends:
+        copy.wait_send()
+
+    @pl.when(z < n_space - 1)
+    def _():
+        rim.wait_send()
+
+    keep.wait()
+
+
+def forward_kernel(
+    sizes, width, own_ref, w_ref, b_ref, g_ref, x_ref, act_ref, dy_ref, db_ref, out_sem, in_sem, local_sem
+):
+    gather_inputs(sizes, own_ref, x_ref, out_sem, in_sem, local_sem)
     sums = [None] * 4
     for t, (k1, k2, k3) in enumerate(TAPS):
         ph, s = phase_of(k2, k3), shift_of(k2, k3)
         part = jnp.dot(
             w_ref[:, t * width : (t + 1) * width],
-            x_ref[k1, :, ph * CELLS : (ph + 1) * CELLS],
+            x_ref[k1, :, :, ph * CELLS : (ph + 1) * CELLS].reshape(width, CELLS),
             preferred_element_type=F32,
         )
         sums[s] = part if sums[s] is None else sums[s] + part
@@ -84,7 +200,9 @@
     slope = 0.5 * (1.0 + th) + 0.5 * u * (1.0 - th * th) * c * (1.0 + 3 * 0.044715 * u * u)
     dy = (g_ref[...].astype(F32) * slope).astype(BF)
     dy_ref[...] = dy
-    db_ref[...] = jnp.sum(dy.astype(F32), axis=1, keepdims=True)
+    db_ref[...] = lax.dot_general(
+        jnp.ones((8, CELLS), BF), dy, (((1,), (1,)), ((), ())), preferred_element_type=F32
+    )
 
 
 def shifted(dy):
@@ -98,7 +216,7 @@
         ph, s = phase_of(k2, k3), shift_of(k2, k3)
         part = lax.dot_general(
             views[s],
-            x_ref[k1, :, ph * CELLS : (ph + 1) * CELLS],
+            x_ref[k1, :, :, ph * CELLS : (ph + 1) * CELLS].reshape(width, CELLS),
             (((1,), (1,)), ((), ())),
             preferred_element_type=F32,
         )
@@ -122,17 +240,121 @@
                     preferred_element_type=F32,
                 )
                 total = part if total is None else total + part
-            gx_ref[plane, :, ph * CELLS : (ph + 1) * CELLS] = total.astype(BF)
-
-
-def call(kernel, out_shape, n_in, flops, moved):
+            gx_ref[:, plane, :, ph * CELLS : (ph + 1) * CELLS] = total.astype(BF).reshape(
+                gx_ref.shape[0], gx_ref.shape[2], CELLS
+            )
+
+
+def share_kernel(
+    sizes, dw_ref, gx_ref, db_ref, all_ref, parts_ref, dbs_ref, out_sem, in_sem, gx_out, gx_in, db_out, db_in, local_sem
+):
+    n_dp, n_space, n_chan = sizes
+    group = n_dp * n_space
+    y, z, c = place()
+    g = y * n_space + z
+    greet(sizes)
+    right = (y, jnp.minimum(z + 1, n_space - 1), c)
+    left = (y, jnp.maximum(z - 1, 0), c)
+    across = (1 - y, z, c)
+
+    def hop(way, device, j, src=None):
+        slot = all_ref.at[y * n_space + j]
+        return send(slot if src is None else src, slot, out_sem.at[way, j], in_sem.at[y * n_space + j], device)
+
+    def arrived(h):
+        send(all_ref.at[h], all_ref.at[h], out_sem.at[2, 0], in_sem.at[h], across).wait_recv()
+
+    locals_ = [
+        pltpu.make_async_copy(dw_ref, all_ref.at[g], local_sem.at[0]),
+        pltpu.make_async_copy(gx_ref.at[c], parts_ref.at[c], local_sem.at[1]),
+        pltpu.make_async_copy(db_ref, dbs_ref.at[g], local_sem.at[2]),
+    ]
+
+    @pl.when(z < n_space - 1)
+    def _():
+        hop(0, right, z, dw_ref).start()
+
+    @pl.when(z > 0)
+    def _():
+        hop(1, left, z, dw_ref).start()
+
+    hop(2, across, z, dw_ref).start()
+    extra = []
+    for o in range(1, n_chan):
+        to = (c + o) % n_chan
+        extra.append(
+            send(gx_ref.at[to], parts_ref.at[c], gx_out.at[o], gx_in.at[o], (y, z, to))
+        )
+    for o in range(1, group):
+        to = (g + o) % group
+        extra.append(
+            send(db_ref, dbs_ref.at[g], db_out.at[o], db_in.at[o], (to // n_space, to % n_space, c))
+        )
+    for copy in extra:
+        copy.start()
+    for copy in locals_:
+        copy.start()
+
+    for d in range(1, n_space):
+        @pl.when(z - d >= 0)
+        def _():
+            j = jnp.maximum(z - d, 0)
+            arrived(y * n_space + j)
+
+            @pl.when(z < n_space - 1)
+            def _():
+                hop(0, right, j).start()
+
+            hop(2, across, j).start()
+
+        @pl.when(z + d < n_space)
+        def _():
+            j = jnp.minimum(z + d, n_space - 1)
+            arrived(y * n_space + j)
+
+            @pl.when(z > 0)
+            def _():
+                hop(1, left, j).start()
+
+            hop(2, across, j).start()
+
+    for o in range(1, n_chan):
+        frm = (c - o + n_chan) % n_chan
+        send(parts_ref.at[frm], parts_ref.at[frm], gx_out.at[o], gx_in.at[o], (y, z, frm)).wait_recv()
+    for o in range(1, group):
+        frm = (g - o + group) % group
+        send(dbs_ref.at[frm], dbs_ref.at[frm], db_out.at[o], db_in.at[o], (frm // n_space, frm % n_space, c)).wait_recv()
+    for j in range(n_space):
+        arrived((1 - y) * n_space + j)
+        hop(2, across, j).wait_send()
+
+        @pl.when((j <= z) & (z < n_space - 1))
+        def _():
+            hop(0, right, j).wait_send()
+
+        @pl.when((j >= z) & (z > 0))
+        def _():
+            hop(1, left, j).wait_send()
+
+    for copy in extra:
+        copy.wait_send()
+    for copy in locals_:
+        copy.wait()
+
+
+def call(kernel, out_shape, n_in, flops, moved, scratch=(), collective_id=None):
     many = isinstance(out_shape, (tuple, list))
     return pl.pallas_call(
         kernel,
         out_shape=out_shape,
         in_specs=[VM] * n_in,
         out_specs=[VM] * len(out_shape) if many else VM,
-        compiler_params=pltpu.CompilerParams(vmem_limit_bytes=48 << 20),
+        scratch_shapes=scratch,
+        compiler_params=pltpu.CompilerParams(
+            vmem_limit_bytes=48 << 20,
+            collective_id=collective_id,
+            has_side_effects=collective_id is not None,
+        ),
         cost_estimate=pl.CostEstimate(flops=flops, bytes_accessed=moved, transcendentals=0),
     )
 
@@ -155,31 +377,58 @@
     own = call(split_kernel, shape(planes * part, cells), 2, 2 * planes * part * cells**2, 1 << 20)(
         volumes.reshape(planes * part, cells), parity
     ).reshape(planes, part, cells)
-    rim = from_behind(own[-1:], "space", 1)
-    x_all = lax.all_gather(jnp.concatenate([rim, own], 0), "chan", axis=1, tiled=True)
+    sizes = tuple(lax.axis_size(a) for a in ("dp", "space", "chan"))
+    group, n_chan = sizes[0] * sizes[1], sizes[2]
+    dma = pltpu.SemaphoreType.DMA
     flops = 2 * 27 * width * filters * CELLS
-    act, dy, db = call(
-        functools.partial(forward_kernel, width),
-        (shape(filters, CELLS), shape(filters, CELLS), shape(filters, 1, dtype=F32)),
+    x_all, act, dy, db = call(
+        functools.partial(forward_kernel, sizes, width),
+        (
+            shape(3, n_chan, part, cells),
+            shape(filters, CELLS),
+            shape(filters, CELLS),
+            shape(8, filters, dtype=F32),
+        ),
         4,
         flops,
-        7 << 20,
-    )(x_all, kernel, bias.reshape(filters, 1), act_grad.reshape(filters, CELLS))
+        10 << 20,
+        scratch=(dma((2, 3, n_chan // 2)), dma((2, n_chan)), dma),
+        collective_id=0,
+    )(own, kernel, bias.reshape(filters, 1), act_grad.reshape(filters, CELLS))
     dy_next = from_behind(dy, "space", -1)
     dw = call(functools.partial(weight_kernel, width), shape(filters, 27 * width), 2, flops, 7 << 20)(
         x_all, dy
     )
-    gx = call(functools.partial(input_kernel, width), shape(planes, width, cells), 3, 2 * flops, 6 << 20)(
+    gx = call(functools.partial(input_kernel, width), shape(n_chan, planes, part, cells), 3, 2 * flops, 6 << 20)(
         kernel, dy, dy_next
     )
     count = batch * lax.axis_size("dp")
     dw_sum = lax.psum_scatter(dw, ("dp", "space"), scatter_dimension=0, tiled=True)
-    dw_all = lax.all_gather(dw_sum, ("dp", "space"), axis=0, tiled=True)
-    grad_w = dw_all.astype(F32) / count
-    grad_b = lax.psum(db[:, 0], ("dp", "space")) / count
-    gx_sum = lax.psum_scatter(gx, "chan", scatter_dimension=1, tiled=True)
+    dw_all, parts, dbs = call(
+        functools.partial(share_kernel, sizes),
+        (
+            shape(group, *dw_sum.shape),
+            shape(n_chan, planes, part, cells),
+            shape(group, 8, filters, dtype=F32),
+        ),
+        3,
+        0,
+        12 << 20,
+        scratch=(
+            dma((3, sizes[1])),
+            dma((group,)),
+            dma((n_chan,)),
+            dma((n_chan,)),
+            dma((group,)),
+            dma((group,)),
+            dma((3,)),
+        ),
+        collective_id=1,
+    )(dw_sum, gx, db)
+    grad_w = dw_all.reshape(filters, 27 * width).astype(F32) / count
+    grad_b = jnp.sum(dbs[:, 0], axis=0) / count
     grad_x = call(merge_kernel, shape(planes * part, cells), 2, 2 * planes * part * cells**2, 1 << 20)(
-        gx_sum.reshape(planes * part, cells), parity
+        parts, parity
     )
     return (
         act.reshape(act_grad.shape),

time: 255 us -> 185 us (0.73)
  waiting for transfers between devices: 185 us -> 76 us
  Pallas kernels: 12.5 us -> 79.5 us
  blocking collectives: 20.2 us -> 0 us
  starting transfers between devices: 6.43 us -> 1.33 us
  other arithmetic: 8.13 us -> 5.15 us
    all_gather x2 -> x0, waiting for transfers between devices: 94.7 us -> none  [the longest x1 64 us: per_device(): dw_all = lax.all_gather(dw_sum, ('dp', 'space'), axis=0, tiled=True)]
    pallas_call x2 -> x3, Pallas kernels: 5.92 us -> 72.8 us  [the longest x1 46.4 us: per_device(): call(functools.partial(share_kernel, sizes), (shape(group, *dw_sum.shape)...]
    psum x1 -> x0, blocking collectives: 20.2 us -> none  [per_device(): grad_b = lax.psum(db[:, 0], ('dp', 'space')) / count]
    reduce_scatter x1 -> x0, waiting for transfers between devices: 12.5 us -> none  [per_device(): gx_sum = lax.psum_scatter(gx, 'chan', scatter_dimension=1, tiled=True)]
    ppermute x2 -> x1, starting transfers between devices: 6.26 us -> 1.29 us  [from_behind(): return lax.ppermute(array, axis, pairs)]
    ppermute x2 -> x1, waiting for transfers between devices: 10.4 us -> 9.05 us  [from_behind(): return lax.ppermute(array, axis, pairs)]
    unnamed x14 -> x15, local copies, waits for them, and re-layouts: 7.63 us -> 7.64 us
  transfers between devices with their start and end apart: 6 -> 2, of which waited for: 6 -> 2; matrix products, arithmetic and copies ran while one was open for 0% -> 0% of each run, Pallas kernels for 1% -> 1%
where the time goes in v1:
time: 185 us; the launch traced here: 184 us
  Pallas kernels  79.5 us (43%)
  waiting for transfers between devices  76 us (41%)
  between operations  14.1 us (8%)
  local copies, waits for them, and re-layouts  8.41 us (5%)
  other arithmetic  5.15 us (3%)
    reduce_scatter x1, waiting for transfers between devices, per_device(): lax.psum_scatter(dw, ('dp', 'space'), scatter_dimension=0, tiled=True)  66.9 us
    pallas_call x1, Pallas kernels, per_device(): call(functools.partial(share_kernel, sizes), (shape(group, *dw_sum.shape)...  46.4 us
    pallas_call x1, Pallas kernels, per_device(): call(functools.partial(forward_kernel, sizes, width), (shape(3, n_chan, p...  24.4 us
    ppermute x1, waiting for transfers between devices, from_behind(): return lax.ppermute(array, axis, pairs)  9.05 us
    unnamed x15, local copies, waits for them, and re-layouts  7.64 us
    pallas_call x1, Pallas kernels, per_device(): call(functools.partial(weight_kernel, width), shape(filters, 27 * width),...  4.34 us
    div x1, other arithmetic, per_device(): grad_w = dw_all.reshape(filters, 27 * width).astype(F32) / count  3.71 us
  transfers between devices with their start and end apart: 2, of which 2 were waited for; matrix products, arithmetic and copies ran while one was open for 0% of the time, Pallas kernels for 1%

profile of v1, /device:TPU:0, one launch (start us, length us, event | category | flops | bytes accessed | tf_op | source)
XLA Modules:
  0.0 184.5 jit_solution(1839881833984023730)
XLA Ops:
  7.2 0.0 copy-start.5
  7.2 0.0 reduce-scatter.2.cloned.1.call-start
  7.2 0.8 copy.8.b_ref
  8.0 0.9 select_convert_fusion.p_ref
  8.9 0.0 copy-start.3
  8.9 1.0 copy-done.3
  9.9 0.7 shard_map.75
  10.6 0.0 copy-done.5
  10.7 24.4 %shard_map.76 = (bf16[3,4,128,1024]{3,2,1,0:T(8,128)(2,1)S(1)}, bf16[128,256]{1,0:T(8,128)(2,1)S(1)}, bf16[128,256]{1,0:T(8,128)(2,1)S(1)}, f32[8,128]{1,0:T(8,128)S(1)}) custom-call(bf16[2,128,1024]{2,1,0:T(8,128)(2,1)S(1)} %bitcast.7, bf16[128,13824]{1,0:T(8,128)(2,1)} %w_ref.3, f32[128,1]{1,0:T(8,128)S(1)} %copy.8.b_ref, bf16[128,256]{1,0:T(8,128)(2,1)S(1)} %bitcast.9), custom_call_target="tpu_custom_call" | custom-call | flops 905969664 | bytes 10485760 | tf_op jit(solution)/shard_map/pallas_call | solution.py:384
  35.0 4.3 %shard_map.77 = bf16[128,13824]{1,0:T(8,128)(2,1)} custom-call(bf16[3,4,128,1024]{3,2,1,0:T(8,128)(2,1)S(1)} %get-tuple-element.12.x_ref, bf16[128,256]{1,0:T(8,128)(2,1)S(1)} %get-tuple-element.13.dy_ref), custom_call_target="tpu_custom_call" | custom-call | flops 905969664 | bytes 7340032 | tf_op jit(solution)/shard_map/pallas_call | solution.py:399
  39.4 0.0 reduce-scatter.2.cloned.1.call-update
  39.4 1.3 collective-permute-start
  40.7 9.1 %collective-permute-done.next_ref = bf16[128,256]{1,0:T(8,128)(2,1)S(1)} collective-permute-done((bf16[128,256]{1,0:T(8,128)(2,1)S(1)}, bf16[128,256]{1,0:T(8,128)(2,1)S(1)}, u32[]{:S(2)}, u32[]{:S(2)}) %collective-permute-start) | collective-permute-done | bytes 65568 | tf_op jit(solution)/shard_map/ppermute | solution.py:369
  49.7 0.0 copy-start
  49.7 2.0 %copy-done = bf16[128,13824]{1,0:T(8,128)(2,1)S(1)} copy-done((bf16[128,13824]{1,0:T(8,128)(2,1)S(1)}, bf16[128,13824]{1,0:T(8,128)(2,1)}, u32[]{:S(2)}) %copy-start) | copy-done | bytes 3538968
  51.8 2.0 %shard_map.78.gx_ref = bf16[4,2,128,1024]{3,2,1,0:T(8,128)(2,1)S(1)} custom-call(bf16[128,13824]{1,0:T(8,128)(2,1)S(1)} %copy-done, bf16[128,256]{1,0:T(8,128)(2,1)S(1)} %get-tuple-element.13.dy_ref, bf16[128,256]{1,0:T(8,128)(2,1)S(1)} %collective-permute-done.next_ref), custom_call_target="tpu_custom_call" | custom-call | flops 1811939328 | bytes 6291456 | tf_op jit(solution)/shard_map/pallas_call | solution.py:402
  53.8 0.0 copy-start.1
  53.8 1.3 copy-done.1
  55.2 66.9 %reduce-scatter.2.cloned.1.call-done.dw_ref = bf16[16,13824]{1,0:T(8,128)(2,1)} async-done(((bf16[128,13824]{1,0:T(8,128)(2,1)}), bf16[16,13824]{1,0:T(8,128)(2,1)}) %reduce-scatter.2.cloned.1.call-update) | async-done | bytes 442384 | tf_op jit(solution)/shard_map/reduce_scatter | solution.py:406
  122.1 0.0 copy-start.2
  122.1 1.6 copy-done.2
  123.7 0.0 copy-start.4
  123.7 1.0 copy-done.4
  124.7 46.4 %shard_map.79 = (bf16[8,16,13824]{2,1,0:T(8,128)(2,1)}, bf16[4,2,128,1024]{3,2,1,0:T(8,128)(2,1)S(1)}, f32[8,8,128]{2,1,0:T(8,128)S(1)}) custom-call(bf16[16,13824]{1,0:T(8,128)(2,1)S(1)} %copy-done.4, bf16[4,2,128,1024]{3,2,1,0:T(8,128)(2,1)S(1)} %copy-done.2, f32[8,128]{1,0:T(8,128)S(1)} %get-tuple-element.14.db_ref), custom_call_target="tpu_custom_call" | custom-call | bytes 12582912 | tf_op jit(solution)/shard_map/pallas_call | solution.py:407
  171.1 0.0 copy-start.6
  171.1 1.7 shard_map.80
  172.8 0.5 broadcast_multiply_fusion
  173.3 0.0 copy-done.6
  173.3 3.7 %convert_multiply_fusion = f32[8,16,13824]{2,1,0:T(8,128)} fusion(bf16[8,16,13824]{2,1,0:T(8,128)(2,1)S(1)} %copy-done.6), kind=kLoop, calls=%fused_computation | loop fusion | flops 3538944 | bytes 10616832 | tf_op jit(solution)/shard_map/div | solution.py:428
  177.0 0.6 copy.10
  (2 shorter events, 0.0 us)
Async XLA Ops:
  7.2 3.5 %copy-start.5 = (bf16[1,1,128,256]{3,2,1,0:T(8,128)(2,1)S(1)}, bf16[1,1,128,256]{3,2,1,0:T(8,128)(2,1)}, u32[]{:S(2)}) copy-start(bf16[1,1,128,256]{3,2,1,0:T(8,128)(2,1)} %param.7) | copy-start | bytes 196612
  7.2 114.9 %reduce-scatter.2.cloned.1.call-start = ((), (), s32[]{:S(2)}) async-start(), calls=%async_computation.1 | async-start | bytes 3981312 | tf_op jit(solution)/shard_map/reduce_scatter | solution.py:406
  8.9 1.0 copy-start.3
  39.4 10.4 %collective-permute-start = (bf16[128,256]{1,0:T(8,128)(2,1)S(1)}, bf16[128,256]{1,0:T(8,128)(2,1)S(1)}, u32[]{:S(2)}, u32[]{:S(2)}) collective-permute-start(bf16[128,256]{1,0:T(8,128)(2,1)S(1)} %get-tuple-element.13.dy_ref), channel_id=1, source_target_pairs={{4,0},{8,4},{12,8},{5,1},{9,5},{13,9},{6,2},{10,6},{14,10},{7,3},{... | collective-permute-start | bytes 196616 | tf_op jit(solution)/shard_map/ppermute | solution.py:369
  49.7 2.0 %copy-start = (bf16[128,13824]{1,0:T(8,128)(2,1)S(1)}, bf16[128,13824]{1,0:T(8,128)(2,1)}, u32[]{:S(2)}) copy-start(bf16[128,13824]{1,0:T(8,128)(2,1)} %w_ref.3) | copy-start | bytes 10616836
  53.8 1.3 copy-start.1
  122.1 1.6 copy-start.2
  123.7 1.0 copy-start.4
  171.1 2.2 %copy-start.6 = (bf16[8,16,13824]{2,1,0:T(8,128)(2,1)S(1)}, bf16[8,16,13824]{2,1,0:T(8,128)(2,1)}, u32[]{:S(2)}) copy-start(bf16[8,16,13824]{2,1,0:T(8,128)(2,1)} %get-tuple-element.16) | copy-start | bytes 10616836
Sparse Core Ops, SparseCore 0:
  39.5 82.5 reduce-scatter.1

commit v2 on v1

--- a/solution.py
+++ b/solution.py
@@ -210,21 +210,35 @@
     return [dy] + [backward_shift(wide, s).astype(BF) for s in (1, 2, 3)]
 
 
-def weight_kernel(width, x_ref, dy_ref, dw_ref):
-    views = shifted(dy_ref[...])
+def grads_kernel(sizes, width, x_ref, w_ref, dy_ref, dw_ref, gx_ref, next_ref, out_sem, in_sem):
+    n_space = sizes[1]
+    y, z, c = place()
+    greet(sizes)
+    back = send(dy_ref, next_ref, out_sem, in_sem, (y, jnp.maximum(z - 1, 0), c))
+
+    @pl.when(z > 0)
+    def _():
+        back.start()
+
+    own = shifted(dy_ref[...])
     for t, (k1, k2, k3) in enumerate(TAPS):
         ph, s = phase_of(k2, k3), shift_of(k2, k3)
         part = lax.dot_general(
-            views[s],
+            own[s],
             x_ref[k1, :, :, ph * CELLS : (ph + 1) * CELLS].reshape(width, CELLS),
             (((1,), (1,)), ((), ())),
             preferred_element_type=F32,
         )
         dw_ref[:, t * width : (t + 1) * width] = part.astype(BF)
 
-
-def input_kernel(width, w_ref, dy_ref, next_ref, gx_ref):
-    own = shifted(dy_ref[...])
+    @pl.when(z < n_space - 1)
+    def _():
+        back.wait_recv()
+
+    @pl.when(z == n_space - 1)
+    def _():
+        next_ref[...] = jnp.zeros_like(next_ref)
+
     following = shifted(next_ref[...])
     for plane in range(2):
         for ph in range(4):
@@ -244,9 +258,14 @@
                 gx_ref.shape[0], gx_ref.shape[2], CELLS
             )
 
+    @pl.when(z > 0)
+    def _():
+        back.wait_send()
+
 
 def share_kernel(
-    sizes, dw_ref, gx_ref, db_ref, all_ref, parts_ref, dbs_ref, out_sem, in_sem, gx_out, gx_in, db_out, db_in, local_sem
+    sizes, dw_ref, gx_ref, db_ref, all_ref, parts_ref, dbs_ref, y_ref, r_ref, l_ref, s_ref,
+    out_sem, in_sem, gx_out, gx_in, db_out, db_in, local_sem, y_out, y_in, z_out, r_in, l_in
 ):
     n_dp, n_space, n_chan = sizes
     group = n_dp * n_space
@@ -265,20 +284,33 @@
         send(all_ref.at[h], all_ref.at[h], out_sem.at[2, 0], in_sem.at[h], across).wait_recv()
 
     locals_ = [
-        pltpu.make_async_copy(dw_ref, all_ref.at[g], local_sem.at[0]),
         pltpu.make_async_copy(gx_ref.at[c], parts_ref.at[c], local_sem.at[1]),
         pltpu.make_async_copy(db_ref, dbs_ref.at[g], local_sem.at[2]),
     ]
 
-    @pl.when(z < n_space - 1)
-    def _():
-        hop(0, right, z, dw_ref).start()
-
-    @pl.when(z > 0)
-    def _():
-        hop(1, left, z, dw_ref).start()
-
-    hop(2, across, z, dw_ref).start()
+    def over(j):
+        return send(dw_ref.at[(1 - y) * n_space + j], y_ref.at[j], y_out.at[j], y_in.at[j], across)
+
+    def rightward(j):
+        return send(s_ref.at[j], r_ref.at[j], z_out.at[j], r_in.at[j], right)
+
+    def leftward(j):
+        return send(s_ref.at[j], l_ref.at[j], z_out.at[j], l_in.at[j], left)
+
+    def both(j):
+        over(j).wait_recv()
+        return dw_ref[y * n_space + j].astype(F32) + y_ref[j].astype(F32)
+
+    for d in range(n_space - 1, 0, -1):
+        @pl.when(z + d < n_space)
+        def _():
+            over(jnp.minimum(z + d, n_space - 1)).start()
+
+        @pl.when(z - d >= 0)
+        def _():
+            over(jnp.maximum(z - d, 0)).start()
+
+    over(z).start()
     extra = []
     for o in range(1, n_chan):
         to = (c + o) % n_chan
@@ -294,6 +326,67 @@
         copy.start()
     for copy in locals_:
         copy.start()
+
+    for d in range(n_space - 1, 0, -1):
+        @pl.when(z + d < n_space)
+        def _():
+            j = jnp.minimum(z + d, n_space - 1)
+            mine = both(j)
+
+            @pl.when(z == 0)
+            def _():
+                s_ref[j] = mine.astype(BF)
+
+            @pl.when(z > 0)
+            def _():
+                rightward(j).wait_recv()
+                s_ref[j] = (mine + r_ref[j].astype(F32)).astype(BF)
+
+            rightward(j).start()
+
+        @pl.when(z - d >= 0)
+        def _():
+            j = jnp.maximum(z - d, 0)
+            mine = both(j)
+
+            @pl.when(z == n_space - 1)
+            def _():
+                s_ref[j] = mine.astype(BF)
+
+            @pl.when(z < n_space - 1)
+            def _():
+                leftward(j).wait_recv()
+                s_ref[j] = (mine + l_ref[j].astype(F32)).astype(BF)
+
+            leftward(j).start()
+
+    @pl.when(z == 0)
+    def _():
+        r_ref[z] = jnp.zeros_like(r_ref[z])
+
+    @pl.when(z == n_space - 1)
+    def _():
+        l_ref[z] = jnp.zeros_like(l_ref[z])
+
+    @pl.when(z > 0)
+    def _():
+        rightward(z).wait_recv()
+
+    @pl.when(z < n_space - 1)
+    def _():
+        leftward(z).wait_recv()
+
+    all_ref[g] = (both(z) + r_ref[z].astype(F32) + l_ref[z].astype(F32)).astype(BF)
+
+    @pl.when(z < n_space - 1)
+    def _():
+        hop(0, right, z).start()
+
+    @pl.when(z > 0)
+    def _():
+        hop(1, left, z).start()
+
+    hop(2, across, z).start()
 
     for d in range(1, n_space):
         @pl.when(z - d >= 0)
@@ -335,6 +428,16 @@
         @pl.when((j >= z) & (z > 0))
         def _():
             hop(1, left, j).wait_send()
+
+        over(j).wait_send()
+
+        @pl.when(j > z)
+        def _():
+            rightward(j).wait_send()
+
+        @pl.when(j < z)
+        def _():
+            leftward(j).wait_send()
 
     for copy in extra:
         copy.wait_send()
@@ -361,12 +464,6 @@
 
 def shape(*dims, dtype=BF):
     return jax.ShapeDtypeStruct(dims, dtype)
-
-
-def from_behind(array, axis, by):
-    size = lax.axis_size(axis)
-    pairs = [(i, i + by) for i in range(size) if 0 <= i + by < size]
-    return lax.ppermute(array, axis, pairs)
 
 
 def per_device(volumes, kernel, bias, act_grad):
@@ -395,19 +492,22 @@
         scratch=(dma((2, 3, n_chan // 2)), dma((2, n_chan)), dma),
         collective_id=0,
     )(own, kernel, bias.reshape(filters, 1), act_grad.reshape(filters, CELLS))
-    dy_next = from_behind(dy, "space", -1)
-    dw = call(functools.partial(weight_kernel, width), shape(filters, 27 * width), 2, flops, 7 << 20)(
-        x_all, dy
-    )
-    gx = call(functools.partial(input_kernel, width), shape(n_chan, planes, part, cells), 3, 2 * flops, 6 << 20)(
-        kernel, dy, dy_next
-    )
-    count = batch * lax.axis_size("dp")
-    dw_sum = lax.psum_scatter(dw, ("dp", "space"), scatter_dimension=0, tiled=True)
+    dw, gx = call(
+        functools.partial(grads_kernel, sizes, width),
+        (shape(filters, 27 * width), shape(n_chan, planes, part, cells)),
+        3,
+        3 * flops,
+        12 << 20,
+        scratch=(pltpu.VMEM((filters, CELLS), BF), dma, dma),
+        collective_id=2,
+    )(x_all, kernel, dy)
+    count = batch * sizes[0]
+    rows = filters // group
+    slots = pltpu.VMEM((sizes[1], rows, 27 * width), BF)
     dw_all, parts, dbs = call(
         functools.partial(share_kernel, sizes),
         (
-            shape(group, *dw_sum.shape),
+            shape(group, rows, 27 * width),
             shape(n_chan, planes, part, cells),
             shape(group, 8, filters, dtype=F32),
         ),
@@ -415,6 +515,10 @@
         0,
         12 << 20,
         scratch=(
+            slots,
+            slots,
+            slots,
+            slots,
             dma((3, sizes[1])),
             dma((group,)),
             dma((n_chan,)),
@@ -422,9 +526,14 @@
             dma((group,)),
             dma((group,)),
             dma((3,)),
+            dma((sizes[1],)),
+            dma((sizes[1],)),
+            dma((sizes[1],)),
+            dma((sizes[1],)),
+            dma((sizes[1],)),
         ),
         collective_id=1,
-    )(dw_sum, gx, db)
+    )(dw.reshape(group, rows, 27 * width), gx, db)
     grad_w = dw_all.reshape(filters, 27 * width).astype(F32) / count
     grad_b = jnp.sum(dbs[:, 0], axis=0) / count
     grad_x = call(merge_kernel, shape(planes * part, cells), 2, 2 * planes * part * cells**2, 1 << 20)(

time: 185 us -> 136 us (0.74)
  waiting for transfers between devices: 76 us -> 0 us
  Pallas kernels: 79.5 us -> 127 us
  between operations: 14.1 us -> 0.71 us
  local copies, waits for them, and re-layouts: 8.41 us -> 2.47 us
    reduce_scatter x1 -> x0, waiting for transfers between devices: 66.9 us -> none  [per_device(): lax.psum_scatter(dw, ('dp', 'space'), scatter_dimension=0, tiled=True)]
    pallas_call x3 -> x2, Pallas kernels: 52.8 us -> 101 us  [the longest x1 85.6 us: per_device(): call(functools.partial(share_kernel, sizes), (shape(group, rows, 27 * wid...]
    ppermute x1 -> x0, waiting for transfers between devices: 9.05 us -> none  [from_behind(): return lax.ppermute(array, axis, pairs)]
    unnamed x15 -> x7, local copies, waits for them, and re-layouts: 7.64 us -> 1.67 us
  transfers between devices with their start and end apart: 2 -> 0, of which waited for: 2 -> 0; matrix products, arithmetic and copies ran while one was open for 0% -> 0% of each run, Pallas kernels for 1% -> 0%
where the time goes in v2:
time: 136 us
  Pallas kernels  127 us (93%)
  other arithmetic  5.15 us (4%)
  local copies, waits for them, and re-layouts  2.47 us (2%)
    pallas_call x1, Pallas kernels, per_device(): call(functools.partial(share_kernel, sizes), (shape(group, rows, 27 * wid...  85.6 us
    pallas_call x1, Pallas kernels, per_device(): call(functools.partial(forward_kernel, sizes, width), (shape(3, n_chan, p...  24.3 us
    pallas_call x1, Pallas kernels, per_device(): call(functools.partial(grads_kernel, sizes, width), (shape(filters, 27 *...  15.1 us
    div x1, other arithmetic, per_device(): grad_w = dw_all.reshape(filters, 27 * width).astype(F32) / count  3.71 us

profile of v2, /device:TPU:0, one launch (start us, length us, event | category | flops | bytes accessed | tf_op | source)
XLA Modules:
  0.0 135.8 jit_solution(6113304077028741444)
XLA Ops:
  0.6 0.0 copy-start.1
  0.7 0.8 copy.8.b_ref
  1.4 0.9 select_convert_fusion.p_ref
  2.3 0.0 copy-start
  2.4 1.0 copy-done
  3.4 0.7 shard_map.75
  4.1 0.0 copy-done.1
  4.1 24.3 %shard_map.76 = (bf16[3,4,128,1024]{3,2,1,0:T(8,128)(2,1)S(1)}, bf16[128,256]{1,0:T(8,128)(2,1)S(1)}, bf16[128,256]{1,0:T(8,128)(2,1)S(1)}, f32[8,128]{1,0:T(8,128)S(1)}) custom-call(bf16[2,128,1024]{2,1,0:T(8,128)(2,1)S(1)} %bitcast.8, bf16[128,13824]{1,0:T(8,128)(2,1)} %w_ref.3, f32[128,1]{1,0:T(8,128)S(1)} %copy.8.b_ref, bf16[128,256]{1,0:T(8,128)(2,1)S(1)} %bitcast.10), custom_call_target="tpu_custom_call" | custom-call | flops 905969664 | bytes 10485760 | tf_op jit(solution)/shard_map/pallas_call | solution.py:481
  28.4 15.1 %shard_map.77 = (bf16[128,13824]{1,0:T(8,128)(2,1)}, bf16[4,2,128,1024]{3,2,1,0:T(8,128)(2,1)S(1)}) custom-call(bf16[3,4,128,1024]{3,2,1,0:T(8,128)(2,1)S(1)} %get-tuple-element.14.x_ref, bf16[128,13824]{1,0:T(8,128)(2,1)} %w_ref.3, bf16[128,256]{1,0:T(8,128)(2,1)S(1)} %get-tuple-element.15.dy_ref), custom_call_target="tpu_custom_call" | custom-call | flops 2717908992 | bytes 12582912 | tf_op jit(solution)/shard_map/pallas_call | solution.py:495
  43.6 85.6 %shard_map.78 = (bf16[8,16,13824]{2,1,0:T(8,128)(2,1)}, bf16[4,2,128,1024]{3,2,1,0:T(8,128)(2,1)S(1)}, f32[8,8,128]{2,1,0:T(8,128)S(1)}) custom-call(bf16[8,16,13824]{2,1,0:T(8,128)(2,1)} %bitcast.13, bf16[4,2,128,1024]{3,2,1,0:T(8,128)(2,1)S(1)} %get-tuple-element.17.gx_ref, f32[8,128]{1,0:T(8,128)S(1)} %get-tuple-element.18.db_ref), custom_call_target="tpu_custom_call" | custom-call | bytes 12582912 | tf_op jit(solution)/shard_map/pallas_call | solution.py:507
  129.2 0.0 copy-start.2
  129.2 1.7 %shard_map.79 = bf16[256,1024]{1,0:T(8,128)(2,1)} custom-call(bf16[4,2,128,1024]{3,2,1,0:T(8,128)(2,1)S(1)} %get-tuple-element.19.v_ref, bf16[1024,1024]{1,0:T(8,128)(2,1)S(1)} %select_convert_fusion.p_ref), custom_call_target="tpu_custom_call" | custom-call | flops 536870912 | bytes 1048576 | tf_op jit(solution)/shard_map/pallas_call | solution.py:539
  130.9 0.5 broadcast_multiply_fusion
  131.4 0.0 copy-done.2
  131.4 3.7 %convert_multiply_fusion = f32[8,16,13824]{2,1,0:T(8,128)} fusion(bf16[8,16,13824]{2,1,0:T(8,128)(2,1)S(1)} %copy-done.2), kind=kLoop, calls=%fused_computation | loop fusion | flops 3538944 | bytes 10616832 | tf_op jit(solution)/shard_map/div | solution.py:537
  135.1 0.6 copy.10
  (2 shorter events, 0.0 us)
Async XLA Ops:
  0.6 3.5 %copy-start.1 = (bf16[1,1,128,256]{3,2,1,0:T(8,128)(2,1)S(1)}, bf16[1,1,128,256]{3,2,1,0:T(8,128)(2,1)}, u32[]{:S(2)}) copy-start(bf16[1,1,128,256]{3,2,1,0:T(8,128)(2,1)} %param.7) | copy-start | bytes 196612
  2.3 1.0 copy-start
  129.2 2.2 %copy-start.2 = (bf16[8,16,13824]{2,1,0:T(8,128)(2,1)S(1)}, bf16[8,16,13824]{2,1,0:T(8,128)(2,1)}, u32[]{:S(2)}) copy-start(bf16[8,16,13824]{2,1,0:T(8,128)(2,1)} %get-tuple-element.20) | copy-start | bytes 10616836

commit v3 on v2

--- a/solution.py
+++ b/solution.py
@@ -264,7 +264,7 @@
 
 
 def share_kernel(
-    sizes, dw_ref, gx_ref, db_ref, all_ref, parts_ref, dbs_ref, y_ref, r_ref, l_ref, s_ref,
+    sizes, dw_ref, gx_ref, db_ref, p_ref, all_ref, merged_ref, dbs_ref, parts_ref, y_ref, r_ref, l_ref, s_ref,
     out_sem, in_sem, gx_out, gx_in, db_out, db_in, local_sem, y_out, y_in, z_out, r_in, l_in
 ):
     n_dp, n_space, n_chan = sizes
@@ -387,6 +387,11 @@
         hop(1, left, z).start()
 
     hop(2, across, z).start()
+    for o in range(1, n_chan):
+        frm = (c - o + n_chan) % n_chan
+        send(parts_ref.at[frm], parts_ref.at[frm], gx_out.at[o], gx_in.at[o], (y, z, frm)).wait_recv()
+    locals_[0].wait()
+    merge_kernel(parts_ref, p_ref, merged_ref)
 
     for d in range(1, n_space):
         @pl.when(z - d >= 0)
@@ -411,9 +416,6 @@
 
             hop(2, across, j).start()
 
-    for o in range(1, n_chan):
-        frm = (c - o + n_chan) % n_chan
-        send(parts_ref.at[frm], parts_ref.at[frm], gx_out.at[o], gx_in.at[o], (y, z, frm)).wait_recv()
     for o in range(1, group):
         frm = (g - o + group) % group
         send(dbs_ref.at[frm], dbs_ref.at[frm], db_out.at[o], db_in.at[o], (frm // n_space, frm % n_space, c)).wait_recv()
@@ -441,8 +443,7 @@
 
     for copy in extra:
         copy.wait_send()
-    for copy in locals_:
-        copy.wait()
+    locals_[1].wait()
 
 
 def call(kernel, out_shape, n_in, flops, moved, scratch=(), collective_id=None):
@@ -504,17 +505,18 @@
     count = batch * sizes[0]
     rows = filters // group
     slots = pltpu.VMEM((sizes[1], rows, 27 * width), BF)
-    dw_all, parts, dbs = call(
+    dw_all, grad_x, dbs = call(
         functools.partial(share_kernel, sizes),
         (
             shape(group, rows, 27 * width),
-            shape(n_chan, planes, part, cells),
+            shape(planes * part, cells),
             shape(group, 8, filters, dtype=F32),
         ),
-        3,
-        0,
+        4,
+        2 * planes * part * cells**2,
         12 << 20,
         scratch=(
+            pltpu.VMEM((n_chan, planes, part, cells), BF),
             slots,
             slots,
             slots,
@@ -533,12 +535,9 @@
             dma((sizes[1],)),
         ),
         collective_id=1,
-    )(dw.reshape(group, rows, 27 * width), gx, db)
+    )(dw.reshape(group, rows, 27 * width), gx, db, parity)
     grad_w = dw_all.reshape(filters, 27 * width).astype(F32) / count
     grad_b = jnp.sum(dbs[:, 0], axis=0) / count
-    grad_x = call(merge_kernel, shape(planes * part, cells), 2, 2 * planes * part * cells**2, 1 << 20)(
-        parts, parity
-    )
     return (
         act.reshape(act_grad.shape),
         grad_x.reshape(volumes.shape),

time: 136 us -> 137 us (level)
  other arithmetic: 5.15 us -> 7.11 us
    div x1, other arithmetic: 3.71 us -> 5.67 us  [per_device(): grad_w = dw_all.reshape(filters, 27 * width).astype(F32) / count]
    pallas_call x1 -> x0, Pallas kernels: 1.66 us -> none  [per_device(): call(merge_kernel, shape(planes * part, cells), 2, 2 * planes * part * ce...]
where the time goes in v3:
time: 137 us
  Pallas kernels  126 us (92%)
  other arithmetic  7.11 us (5%)
  local copies, waits for them, and re-layouts  3.26 us (2%)
    pallas_call x1, Pallas kernels, per_device(): call(functools.partial(share_kernel, sizes), (shape(group, rows, 27 * wid...  85.6 us
    pallas_call x1, Pallas kernels, per_device(): call(functools.partial(forward_kernel, sizes, width), (shape(3, n_chan, p...  24.3 us
    pallas_call x1, Pallas kernels, per_device(): call(functools.partial(grads_kernel, sizes, width), (shape(filters, 27 *...  15.1 us
    div x1, other arithmetic, per_device(): grad_w = dw_all.reshape(filters, 27 * width).astype(F32) / count  5.67 us

profile of v3, /device:TPU:0, one launch (start us, length us, event | category | flops | bytes accessed | tf_op | source)
XLA Modules:
  0.0 136.8 jit_solution(17379716286893016640)
XLA Ops:
  0.6 0.0 copy-start.1
  0.7 0.8 copy.8.b_ref
  1.4 0.9 select_convert_fusion.p_ref
  2.3 0.0 copy-start
  2.4 1.0 copy-done
  3.4 0.7 shard_map.75
  4.1 0.0 copy-done.1
  4.1 24.3 %shard_map.76 = (bf16[3,4,128,1024]{3,2,1,0:T(8,128)(2,1)S(1)}, bf16[128,256]{1,0:T(8,128)(2,1)S(1)}, bf16[128,256]{1,0:T(8,128)(2,1)S(1)}, f32[8,128]{1,0:T(8,128)S(1)}) custom-call(bf16[2,128,1024]{2,1,0:T(8,128)(2,1)S(1)} %bitcast.8, bf16[128,13824]{1,0:T(8,128)(2,1)} %w_ref.3, f32[128,1]{1,0:T(8,128)S(1)} %copy.8.b_ref, bf16[128,256]{1,0:T(8,128)(2,1)S(1)} %bitcast.11), custom_call_target="tpu_custom_call" | custom-call | flops 905969664 | bytes 10485760 | tf_op jit(solution)/shard_map/pallas_call | solution.py:482
  28.4 15.1 %shard_map.77 = (bf16[128,13824]{1,0:T(8,128)(2,1)}, bf16[4,2,128,1024]{3,2,1,0:T(8,128)(2,1)S(1)}) custom-call(bf16[3,4,128,1024]{3,2,1,0:T(8,128)(2,1)S(1)} %get-tuple-element.14.x_ref, bf16[128,13824]{1,0:T(8,128)(2,1)} %w_ref.3, bf16[128,256]{1,0:T(8,128)(2,1)S(1)} %get-tuple-element.15.dy_ref), custom_call_target="tpu_custom_call" | custom-call | flops 2717908992 | bytes 12582912 | tf_op jit(solution)/shard_map/pallas_call | solution.py:496
  43.5 85.6 %shard_map.78 = (bf16[8,16,13824]{2,1,0:T(8,128)(2,1)}, bf16[256,1024]{1,0:T(8,128)(2,1)S(1)}, f32[8,8,128]{2,1,0:T(8,128)S(1)}) custom-call(bf16[8,16,13824]{2,1,0:T(8,128)(2,1)} %bitcast.14, bf16[4,2,128,1024]{3,2,1,0:T(8,128)(2,1)S(1)} %get-tuple-element.17.gx_ref, f32[8,128]{1,0:T(8,128)S(1)} %get-tuple-element.18.db_ref, ...), custom_call_target="tpu_custom_call" | custom-call | flops 536870912 | bytes 12582912 | tf_op jit(solution)/shard_map/pallas_call | solution.py:508
  129.2 0.5 broadcast_multiply_fusion
  129.7 5.7 %convert_multiply_fusion = f32[8,16,13824]{2,1,0:T(8,128)} fusion(bf16[8,16,13824]{2,1,0:T(8,128)(2,1)} %get-tuple-element.20), kind=kLoop, calls=%fused_computation | loop fusion | flops 3538944 | bytes 10616832 | tf_op jit(solution)/shard_map/div | solution.py:539
  135.4 0.6 copy.11
  136.0 0.8 copy.12
  (2 shorter events, 0.0 us)
Async XLA Ops:
  0.6 3.5 %copy-start.1 = (bf16[1,1,128,256]{3,2,1,0:T(8,128)(2,1)S(1)}, bf16[1,1,128,256]{3,2,1,0:T(8,128)(2,1)}, u32[]{:S(2)}) copy-start(bf16[1,1,128,256]{3,2,1,0:T(8,128)(2,1)} %param.7) | copy-start | bytes 196612
  2.3 1.0 copy-start
